TPU v7x, 32 devices: a whole 2x2x4 slice. The times are simulated.
32 devices in a mesh: fsdp: 2 (over core), ctx: 4 (over y, x), tp: 4 (over z).
Axes of the slice: x: 2, y: 2, z: 4, core: 2. Of those that a mesh axis runs over, the one named last changes fastest.
Arguments:
- tokens: bfloat16 [4096, 2048], P(('fsdp', 'ctx')), may hold values from -6 to 6
- attn_gain: bfloat16 [2048], P(('fsdp', 'ctx')), may hold values from 0.099609375 to 1.8984375
- w_query: bfloat16 [2048, 2048], P(('fsdp', 'ctx'), 'tp'), may hold values from -0.125 to 0.125
- w_key: bfloat16 [2048, 256], P(('fsdp', 'ctx'), 'tp'), may hold values from -0.125 to 0.125
- w_value: bfloat16 [2048, 256], P(('fsdp', 'ctx'), 'tp'), may hold values from -0.125 to 0.125
- w_out: bfloat16 [2048, 2048], P('tp', ('fsdp', 'ctx')), may hold values from -1 to 1
- mlp_gain: bfloat16 [2048], P(('fsdp', 'ctx')), may hold values from 0.099609375 to 1.8984375
- w_gate: bfloat16 [2048, 5632], P(('fsdp', 'ctx'), 'tp'), may hold values from -0.125 to 0.125
- w_up: bfloat16 [2048, 5632], P(('fsdp', 'ctx'), 'tp'), may hold values from -0.125 to 0.125
- w_down: bfloat16 [5632, 2048], P('tp', ('fsdp', 'ctx')), may hold values from -0.15625 to 0.15625
- cotangent: bfloat16 [4096, 2048], P(('fsdp', 'ctx')), may hold values from -6 to 6
- positions: int32 [4096], P(('fsdp', 'ctx')), may hold values from 0 to 1023, as said below
- segments: int32 [4096], P(('fsdp', 'ctx')), may hold values from 0 to 4095, as said below
Outputs:
- output: bfloat16 [4096, 2048], P(('fsdp', 'ctx'))
- input_grad: bfloat16 [4096, 2048], P(('fsdp', 'ctx'))
- attn_gain_grad: float32 [2048], P(('fsdp', 'ctx'))
- w_query_grad: float32 [2048, 2048], P(('fsdp', 'ctx'), 'tp')
- w_key_grad: float32 [2048, 256], P(('fsdp', 'ctx'), 'tp')
- w_value_grad: float32 [2048, 256], P(('fsdp', 'ctx'), 'tp')
- w_out_grad: float32 [2048, 2048], P('tp', ('fsdp', 'ctx'))
- mlp_gain_grad: float32 [2048], P(('fsdp', 'ctx'))
- w_gate_grad: float32 [2048, 5632], P(('fsdp', 'ctx'), 'tp')
- w_up_grad: float32 [2048, 5632], P(('fsdp', 'ctx'), 'tp')
- w_down_grad: float32 [5632, 2048], P('tp', ('fsdp', 'ctx'))
Inputs may be any that keep to these rules, and one draw needn't show every extreme that they name: Every sequence is cut into 8 stretches of 128 consecutive positions, laid in increasing order inside a stretch; its stretches lie on one index of fsdp, two on each index of ctx, in an order drawn from the seed; each device holds 4 stretches, those of one sequence side by side. `segments`: A document is a run of consecutive positions of one sequence with one number, 200 to 2000 long except the last of a sequence, which may be shorter; documents of different sequences have different numbers.
All inputs are finite; a program needn't handle non-finite values.
Results may differ from a plain program's by a relative error of at most 0.025.
Values may be sent and summed in bfloat16 or wider, within the bound.
A program may use at most 192 MiB of HBM per device.

v0:
```python
import jax
import jax.numpy as jnp
from jax import lax
from jax.sharding import PartitionSpec as P

H = 32
KVH = 4
HD = 64


EPSILON = 1e-05
THETA_BASE = 10000.0
MASKED_SCORE = -1e30


def shifted(value, axis, steps):
    count = lax.axis_size(axis)
    pairs = [(source, (source + steps) % count) for source in range(count)]
    return lax.ppermute(value, axis, pairs)


def rope_tables(token_pos, half_size):
    frequency = THETA_BASE ** (-jnp.arange(half_size, dtype=jnp.float32) / half_size)
    angles = token_pos.astype(jnp.float32)[:, None] * frequency[None, :]
    return (jnp.cos(angles), jnp.sin(angles))


def rotate(head_rows, cosine, sine):
    half_size = head_rows.shape[-1] // 2
    first_half = head_rows[..., :half_size]
    second_half = head_rows[..., half_size:]
    cos_rows = cosine[:, None, :]
    sin_rows = sine[:, None, :]
    return jnp.concatenate(
        [
            first_half * cos_rows - second_half * sin_rows,
            second_half * cos_rows + first_half * sin_rows,
        ],
        axis=-1,
    )


def rotate_back(head_rows, cosine, sine):
    half_size = head_rows.shape[-1] // 2
    first_half = head_rows[..., :half_size]
    second_half = head_rows[..., half_size:]
    cos_rows = cosine[:, None, :]
    sin_rows = sine[:, None, :]
    return jnp.concatenate(
        [
            first_half * cos_rows + second_half * sin_rows,
            second_half * cos_rows - first_half * sin_rows,
        ],
        axis=-1,
    )


def project(left_side, right_side):
    return jnp.dot(left_side, right_side, preferred_element_type=jnp.float32)


def project_back(left_side, right_side):
    return lax.dot_general(
        left_side, right_side, (((1,), (1,)), ((), ())), preferred_element_type=jnp.float32
    )


def weight_grad(left_side, right_side):
    return lax.dot_general(
        left_side, right_side, (((0,), (0,)), ((), ())), preferred_element_type=jnp.float32
    )


def rms_norm(rows_in, gain_vec):
    inv_rms = lax.rsqrt(jnp.mean(rows_in * rows_in, axis=-1, keepdims=True) + EPSILON)
    unit_rows = rows_in * inv_rms
    return (unit_rows * gain_vec, unit_rows, inv_rms)


def rms_norm_back(gradient, gain_vec, unit_rows, inv_rms):
    gain_grad = jnp.sum(gradient * unit_rows, axis=0)
    scaled_grad = gradient * gain_vec
    return (
        inv_rms
        * (scaled_grad - unit_rows * jnp.mean(scaled_grad * unit_rows, axis=-1, keepdims=True)),
        gain_grad,
    )


def pair_mask(query_pos, query_seg, key_pos, key_seg):
    return (query_seg[:, None] == key_seg[None, :]) & (key_pos[None, :] <= query_pos[:, None])


def split_block(kv_block, kv_heads):
    key_rows = kv_block[:, : kv_heads * HD].reshape(-1, kv_heads, HD)
    value_rows = kv_block[:, kv_heads * HD :].reshape(-1, kv_heads, HD)
    return (key_rows, value_rows)


def attend_block(state_in, queries, kv_block, visible):
    row_top, row_total, output_sum = state_in
    key_rows, value_rows = split_block(kv_block, queries.shape[1])
    scores = jnp.einsum(
        "qkgd,pkd->kgqp", queries, key_rows, preferred_element_type=jnp.float32
    ) * HD ** (-0.5)
    scores = jnp.where(visible, scores, MASKED_SCORE)
    new_top = jnp.maximum(row_top, jnp.max(scores, axis=-1))
    weights = jnp.where(visible, jnp.exp(scores - new_top[..., None]), 0.0)
    decay_factor = jnp.exp(row_top - new_top)
    row_total = row_total * decay_factor + jnp.sum(weights, axis=-1)
    mixed_heads = jnp.einsum(
        "kgqp,pkd->qkgd",
        weights.astype(jnp.bfloat16),
        value_rows,
        preferred_element_type=jnp.float32,
    )
    output_sum = output_sum * jnp.transpose(decay_factor, (2, 0, 1))[..., None] + mixed_heads
    return (new_top, row_total, output_sum)


def block_grads(queries, out_grad, kv_block, visible, log_total, delta_rows):
    key_rows, value_rows = split_block(kv_block, queries.shape[1])
    scale_factor = HD ** (-0.5)
    scores = (
        jnp.einsum("qkgd,pkd->kgqp", queries, key_rows, preferred_element_type=jnp.float32)
        * scale_factor
    )
    probs_full = jnp.where(
        visible, jnp.exp(jnp.where(visible, scores, MASKED_SCORE) - log_total[..., None]), 0.0
    )
    value_grad = jnp.einsum(
        "kgqp,qkgd->pkd",
        probs_full.astype(jnp.bfloat16),
        out_grad,
        preferred_element_type=jnp.float32,
    )
    prob_grad = jnp.einsum(
        "qkgd,pkd->kgqp", out_grad, value_rows, preferred_element_type=jnp.float32
    )
    score_grad = (probs_full * (prob_grad - delta_rows[..., None])).astype(jnp.bfloat16)
    query_grad = (
        jnp.einsum("kgqp,pkd->qkgd", score_grad, key_rows, preferred_element_type=jnp.float32)
        * scale_factor
    )
    key_grad = (
        jnp.einsum("kgqp,qkgd->pkd", score_grad, queries, preferred_element_type=jnp.float32)
        * scale_factor
    )
    block_rows = kv_block.shape[0]
    return (
        query_grad,
        jnp.concatenate(
            [key_grad.reshape(block_rows, -1), value_grad.reshape(block_rows, -1)], axis=-1
        ),
    )


def shards(
    tokens,
    attn_gain,
    w_query,
    w_key,
    w_value,
    w_out,
    mlp_gain,
    w_gate,
    w_up,
    w_down,
    cotangent,
    positions,
    segments,
):
    token_rows = tokens.shape[0]
    gain_one, query_w, key_w, value_w, out_w = (
        lax.all_gather(attn_gain, ("fsdp", "ctx"), axis=0, tiled=True),
        lax.all_gather(w_query, ("fsdp", "ctx"), axis=0, tiled=True),
        lax.all_gather(w_key, ("fsdp", "ctx"), axis=0, tiled=True),
        lax.all_gather(w_value, ("fsdp", "ctx"), axis=0, tiled=True),
        lax.all_gather(w_out, ("fsdp", "ctx"), axis=1, tiled=True),
    )
    gain_two, gate_w, up_w, down_w = (
        lax.all_gather(mlp_gain, ("fsdp", "ctx"), axis=0, tiled=True),
        lax.all_gather(w_gate, ("fsdp", "ctx"), axis=0, tiled=True),
        lax.all_gather(w_up, ("fsdp", "ctx"), axis=0, tiled=True),
        lax.all_gather(w_down, ("fsdp", "ctx"), axis=1, tiled=True),
    )
    head_count = query_w.shape[1] // HD
    kv_heads = key_w.shape[1] // HD
    groups = H // KVH
    cosine, sine = rope_tables(positions, HD // 2)
    token_float = tokens.astype(jnp.float32)
    gain_one_float = gain_one.astype(jnp.float32)
    normed_one, unit_one, inv_one = rms_norm(token_float, gain_one_float)
    normed_low = normed_one.astype(jnp.bfloat16)
    query_lin = project(normed_low, query_w)
    key_lin = project(normed_low, key_w)
    value_low = project(normed_low, value_w).astype(jnp.bfloat16)
    query_rot = rotate(query_lin.reshape(token_rows, head_count, HD), cosine, sine).astype(
        jnp.bfloat16
    )
    key_rot = rotate(key_lin.reshape(token_rows, kv_heads, HD), cosine, sine).astype(jnp.bfloat16)
    queries = query_rot.reshape(token_rows, kv_heads, groups, HD)
    kv_local = jnp.concatenate([key_rot.reshape(token_rows, kv_heads * HD), value_low], axis=-1)
    key_positions, key_segments = (
        lax.all_gather(positions, "ctx", axis=0, tiled=True),
        lax.all_gather(segments, "ctx", axis=0, tiled=True),
    )
    my_index = lax.axis_index("ctx")
    cycle_size = lax.axis_size("ctx")

    def block_marks(source):
        start_row = source * token_rows
        return pair_mask(
            positions,
            segments,
            lax.dynamic_slice_in_dim(key_positions, start_row, token_rows),
            lax.dynamic_slice_in_dim(key_segments, start_row, token_rows),
        )

    start_state = (
        jnp.full((kv_heads, groups, token_rows), MASKED_SCORE, jnp.float32),
        jnp.zeros((kv_heads, groups, token_rows), jnp.float32),
        jnp.zeros((token_rows, kv_heads, groups, HD), jnp.float32),
    )

    def forward_block(state_in, kv_block, source):
        visible = block_marks(source)
        return attend_block(state_in, queries, kv_block, visible)

    def cycle_step(state_in, step_index):
        attn_state, kv_block = state_in
        attn_state = forward_block(attn_state, kv_block, (my_index - step_index) % cycle_size)
        passed = shifted(kv_block, "ctx", 1)
        return ((attn_state, passed), kv_block)

    (attn_state, last_block), kept_blocks = lax.scan(
        cycle_step, (start_state, kv_local), jnp.arange(cycle_size - 1)
    )
    attn_state = forward_block(attn_state, last_block, (my_index + 1) % cycle_size)
    kv_blocks = jnp.concatenate([kept_blocks, last_block[None]], axis=0)
    sources = (my_index - jnp.arange(cycle_size)) % cycle_size
    row_top, row_total, output_sum = attn_state
    attended = output_sum / jnp.transpose(row_total, (2, 0, 1))[..., None]
    log_total = row_top + jnp.log(row_total)
    attended_low = attended.reshape(token_rows, head_count * HD).astype(jnp.bfloat16)
    middle = token_float + lax.psum(project(attended_low, out_w).astype(jnp.bfloat16), "tp").astype(
        jnp.float32
    )
    gain_two_float = gain_two.astype(jnp.float32)
    normed_two, unit_two, inv_two = rms_norm(middle, gain_two_float)
    normed_two_low = normed_two.astype(jnp.bfloat16)
    gate_lin = project(normed_two_low, gate_w)
    up_lin = project(normed_two_low, up_w)
    hidden_low = (jax.nn.silu(gate_lin) * up_lin).astype(jnp.bfloat16)
    result = middle + lax.psum(project(hidden_low, down_w).astype(jnp.bfloat16), "tp").astype(
        jnp.float32
    )
    output = result.astype(jnp.bfloat16)
    hidden_grad = project_back(cotangent, down_w)
    down_w_grad = weight_grad(hidden_low, cotangent)
    sigmoid_gate = jax.nn.sigmoid(gate_lin)
    gate_grad_low = (
        hidden_grad * up_lin * sigmoid_gate * (1.0 + gate_lin * (1.0 - sigmoid_gate))
    ).astype(jnp.bfloat16)
    up_grad_low = (hidden_grad * gate_lin * sigmoid_gate).astype(jnp.bfloat16)
    normed_two_grad = lax.psum(
        (project_back(gate_grad_low, gate_w) + project_back(up_grad_low, up_w)).astype(
            jnp.bfloat16
        ),
        "tp",
    ).astype(jnp.float32)
    gate_w_grad = weight_grad(normed_two_low, gate_grad_low)
    up_w_grad = weight_grad(normed_two_low, up_grad_low)
    norm_back_two, gain_two_grad = rms_norm_back(normed_two_grad, gain_two_float, unit_two, inv_two)
    middle_grad = cotangent.astype(jnp.float32) + norm_back_two
    middle_low = middle_grad.astype(jnp.bfloat16)
    attended_grad_low = project_back(middle_low, out_w).astype(jnp.bfloat16)
    out_w_grad = weight_grad(attended_low, middle_low)
    out_grad = attended_grad_low.reshape(token_rows, kv_heads, groups, HD)
    delta_rows = jnp.transpose(jnp.sum(out_grad.astype(jnp.float32) * attended, axis=-1), (1, 2, 0))

    def backward_block(kv_block, source):
        visible = block_marks(source)
        return block_grads(queries, out_grad, kv_block, visible, log_total, delta_rows)

    query_start = jnp.zeros((token_rows, kv_heads, groups, HD), jnp.float32)

    def back_step(state_in, pieces):
        query_acc, kv_acc = state_in
        query_term, kv_term = backward_block(pieces[0], pieces[1])
        passed = shifted((kv_acc + kv_term).astype(jnp.bfloat16), "ctx", 1).astype(jnp.float32)
        return ((query_acc + query_term, passed), None)

    (query_grad, kv_grad), unused = lax.scan(
        back_step, (query_start, jnp.zeros(kv_local.shape, jnp.float32)), (kv_blocks, sources)
    )
    query_grad_low = (
        rotate_back(query_grad.reshape(token_rows, head_count, HD), cosine, sine)
        .reshape(token_rows, head_count * HD)
        .astype(jnp.bfloat16)
    )
    key_grad_low = (
        rotate_back(kv_grad[:, : kv_heads * HD].reshape(token_rows, kv_heads, HD), cosine, sine)
        .reshape(token_rows, kv_heads * HD)
        .astype(jnp.bfloat16)
    )
    value_grad_low = kv_grad[:, kv_heads * HD :].astype(jnp.bfloat16)
    normed_one_grad = lax.psum(
        (
            project_back(query_grad_low, query_w)
            + project_back(key_grad_low, key_w)
            + project_back(value_grad_low, value_w)
        ).astype(jnp.bfloat16),
        "tp",
    ).astype(jnp.float32)
    query_w_grad = weight_grad(normed_low, query_grad_low)
    key_w_grad = weight_grad(normed_low, key_grad_low)
    value_w_grad = weight_grad(normed_low, value_grad_low)
    norm_back_one, gain_one_grad = rms_norm_back(normed_one_grad, gain_one_float, unit_one, inv_one)
    input_grad = (middle_grad + norm_back_one).astype(jnp.bfloat16)
    summed = (
        lax.psum_scatter(
            gain_one_grad.astype(jnp.bfloat16), ("fsdp", "ctx"), scatter_dimension=0, tiled=True
        ).astype(jnp.float32),
        lax.psum_scatter(
            query_w_grad.astype(jnp.bfloat16), ("fsdp", "ctx"), scatter_dimension=0, tiled=True
        ).astype(jnp.float32),
        lax.psum_scatter(
            key_w_grad.astype(jnp.bfloat16), ("fsdp", "ctx"), scatter_dimension=0, tiled=True
        ).astype(jnp.float32),
        lax.psum_scatter(
            value_w_grad.astype(jnp.bfloat16), ("fsdp", "ctx"), scatter_dimension=0, tiled=True
        ).astype(jnp.float32),
        lax.psum_scatter(
            out_w_grad.astype(jnp.bfloat16), ("fsdp", "ctx"), scatter_dimension=1, tiled=True
        ).astype(jnp.float32),
        lax.psum_scatter(
            gain_two_grad.astype(jnp.bfloat16), ("fsdp", "ctx"), scatter_dimension=0, tiled=True
        ).astype(jnp.float32),
        lax.psum_scatter(
            gate_w_grad.astype(jnp.bfloat16), ("fsdp", "ctx"), scatter_dimension=0, tiled=True
        ).astype(jnp.float32),
        lax.psum_scatter(
            up_w_grad.astype(jnp.bfloat16), ("fsdp", "ctx"), scatter_dimension=0, tiled=True
        ).astype(jnp.float32),
        lax.psum_scatter(
            down_w_grad.astype(jnp.bfloat16), ("fsdp", "ctx"), scatter_dimension=1, tiled=True
        ).astype(jnp.float32),
    )
    return (output, input_grad) + tuple(summed)


def solution(mesh):
    in_specs = (
        P(("fsdp", "ctx"), None),
        P(("fsdp", "ctx")),
        P(("fsdp", "ctx"), "tp"),
        P(("fsdp", "ctx"), "tp"),
        P(("fsdp", "ctx"), "tp"),
        P("tp", ("fsdp", "ctx")),
        P(("fsdp", "ctx")),
        P(("fsdp", "ctx"), "tp"),
        P(("fsdp", "ctx"), "tp"),
        P("tp", ("fsdp", "ctx")),
        P(("fsdp", "ctx"), None),
        P(("fsdp", "ctx")),
        P(("fsdp", "ctx")),
    )
    out_specs = (
        P(("fsdp", "ctx"), None),
        P(("fsdp", "ctx"), None),
        P(("fsdp", "ctx")),
        P(("fsdp", "ctx"), "tp"),
        P(("fsdp", "ctx"), "tp"),
        P(("fsdp", "ctx"), "tp"),
        P("tp", ("fsdp", "ctx")),
        P(("fsdp", "ctx")),
        P(("fsdp", "ctx"), "tp"),
        P(("fsdp", "ctx"), "tp"),
        P("tp", ("fsdp", "ctx")),
    )
    return jax.shard_map(shards, mesh=mesh, in_specs=in_specs, out_specs=out_specs, check_vma=False)
```

profile of v0, /device:TPU:0, one launch (start us, length us, event | category | flops | bytes accessed | tf_op | source)
XLA Modules:
  0.0 1101.4 jit_solution(18198275863524223515)
XLA Ops:
  8.8 9.6 all-gather.1
  19.1 7.9 all-gather.2
  27.9 12.5 %all-gather = bf16[8,1,256]{2,1,0:T(2,128)(2,1)S(1)} all-gather(bf16[1,1,256]{2,1,0:T(2,128)(2,1)S(1)} %reshape.364), channel_id=1, replica_groups=mesh['fsdp'=2,'ctx'=4,'tp'=4] {'fsdp','ctx'}, dimensions={0}, use_global_device_ids=true | all-gather | bytes 4608 | tf_op jit(solution)/shard_map/all_gather | solution.py:175
  42.5 25.8 %all_gather.34 = bf16[2048,64]{0,1:T(8,128)(2,1)S(1)} all-gather(bf16[256,64]{0,1:T(8,128)(2,1)} %param.20), channel_id=1, replica_groups=mesh['fsdp'=2,'ctx'=4,'tp'=4] {'fsdp','ctx'}, dimensions={0}, use_global_device_ids=true | all-gather | bytes 294912 | tf_op jit(solution)/shard_map/all_gather | solution.py:177
  70.4 24.0 %all_gather.35 = bf16[2048,64]{0,1:T(8,128)(2,1)S(1)} all-gather(bf16[256,64]{0,1:T(8,128)(2,1)S(1)} %copy-done.36), channel_id=1, replica_groups=mesh['fsdp'=2,'ctx'=4,'tp'=4] {'fsdp','ctx'}, dimensions={0}, use_global_device_ids=true | all-gather | bytes 294912 | tf_op jit(solution)/shard_map/all_gather | solution.py:178
  95.5 3.5 fusion.126
  100.0 45.5 %while.34 = (s32[]{:T(128)}, f32[1,8,512]{2,1,0:T(8,128)S(1)}, f32[1,8,512]{2,1,0:T(8,128)S(1)}, f32[512,1,8,64]{0,3,2,1:T(8,128)}, bf16[512,128]{0,1:T(8,128)(2...) while((s32[]{:T(128)}, f32[1,8,512]{2,1,0:T(8,128)S(1)}, ...), condition=%wide.region_4.5_spmd.clone, body=%wide.region_1.4_spmd.clone.sunk | while | flops 565731328 | bytes 63848896 | solution.py:236
  107.1 6.8 fusion.193
  123.6 7.0 fusion.193
  137.8 7.0 fusion.193
  153.9 4.4 convolution_convert_fusion.5
  160.1 14.7 %all-gather.3 = bf16[8,1,256]{2,1,0:T(2,128)(2,1)S(1)} all-gather(bf16[1,1,256]{2,1,0:T(2,128)(2,1)S(1)} %reshape.370), channel_id=1, replica_groups=mesh['fsdp'=2,'ctx'=4,'tp'=4] {'fsdp','ctx'}, dimensions={0}, use_global_device_ids=true | all-gather | bytes 4608 | tf_op jit(solution)/shard_map/all_gather | solution.py:182
  174.8 71.9 %all-reduce.8.cloned.1.call-done = bf16[512,2048]{1,0:T(8,128)(2,1)} async-done(((bf16[512,2048]{1,0:T(8,128)(2,1)}), bf16[512,2048]{1,0:T(8,128)(2,1)}) %all-reduce.8.cloned.1.call-update) | async-done | bytes 2097168 | tf_op jit(solution)/shard_map/psum | solution.py:246
  251.6 39.3 %all-gather.14.cloned.1.call-done = bf16[2048,1408]{1,0:T(8,128)(2,1)} async-done(((bf16[256,1408]{1,0:T(8,128)(2,1)}), bf16[2048,1408]{1,0:T(8,128)(2,1)}) %all-gather.14.cloned.1.call-update) | async-done | bytes 5767184 | tf_op jit(solution)/shard_map/all_gather | solution.py:183
  290.9 8.2 fusion.127
  299.1 37.0 %all-gather.16.cloned.1.call-done = bf16[2048,1408]{1,0:T(8,128)(2,1)} async-done(((bf16[256,1408]{1,0:T(8,128)(2,1)}), bf16[2048,1408]{1,0:T(8,128)(2,1)}) %all-gather.16.cloned.1.call-update) | async-done | bytes 5767184 | tf_op jit(solution)/shard_map/all_gather | solution.py:184
  336.2 8.3 fusion.128
  344.4 38.0 %all-gather.18.cloned.1.call-done = bf16[1408,2048]{1,0:T(8,128)(2,1)} async-done(((bf16[1408,256]{1,0:T(8,128)(2,1)}), bf16[1408,2048]{1,0:T(8,128)(2,1)}) %all-gather.18.cloned.1.call-update) | async-done | bytes 5767184 | tf_op jit(solution)/shard_map/all_gather | solution.py:185
  382.4 10.4 multiply_convert_fusion.1
  392.8 6.6 fusion.129
  399.5 4.7 add_convert_fusion.1
  405.8 85.0 %all-reduce.10.cloned.1.call-done = bf16[512,2048]{1,0:T(8,128)(2,1)} async-done(((bf16[512,2048]{1,0:T(8,128)(2,1)}), bf16[512,2048]{1,0:T(8,128)(2,1)}) %all-reduce.10.cloned.1.call-update) | async-done | bytes 2097168 | tf_op jit(solution)/shard_map/psum | solution.py:266
  490.9 3.9 fusion.65
  495.0 4.7 convolution_convert_fusion.9
  501.0 84.5 %while.35 = (s32[]{:T(128)}, f32[512,1,8,64]{0,3,2,1:T(8,128)}, f32[512,128]{0,1:T(8,128)S(1)}, bf16[4,512,128]{1,2,0:T(8,128)(2,1)}, s32[512]{0:T(512)S(1)}, /*...) while((s32[]{:T(128)}, f32[512,1,8,64]{0,3,2,1:T(8,128)}, ...), condition=%wide.region_14.15_spmd.clone, body=%wide.region_13.14_spmd.clone.sunk | while | flops 1369276416 | bytes 45089044 | solution.py:294
  506.8 3.4 fusion.204
  510.3 4.4 fusion.202
  528.2 3.4 fusion.204
  531.6 4.4 fusion.202
  549.2 3.4 fusion.204
  552.6 4.4 fusion.202
  570.2 3.4 fusion.204
  573.7 4.4 fusion.202
  591.8 6.6 convolution_convert_fusion.3
  599.8 4.2 convolution_convert_fusion.4
  604.1 7.9 convolution_convert_fusion.6
  617.1 8.0 convolution_convert_fusion.2
  625.4 7.9 convolution_convert_fusion.1
  633.4 7.7 convolution_convert_fusion
  644.4 13.2 %reduce-scatter.12.cloned.1.call-done = bf16[256,64]{0,1:T(8,128)(2,1)} async-done(((bf16[2048,64]{0,1:T(8,128)(2,1)}), bf16[256,64]{0,1:T(8,128)(2,1)}) %reduce-scatter.12.cloned.1.call-update) | async-done | bytes 32784 | tf_op jit(solution)/shard_map/reduce_scatter | solution.py:331
  659.0 43.0 %reduce-scatter.14.cloned.1.call-done = bf16[512,256]{1,0:T(8,128)(2,1)} async-done(((bf16[512,2048]{1,0:T(8,128)(2,1)}), bf16[512,256]{1,0:T(8,128)(2,1)}) %reduce-scatter.14.cloned.1.call-update) | async-done | bytes 262160 | tf_op jit(solution)/shard_map/reduce_scatter | solution.py:334
  703.8 43.1 %reduce-scatter.8.cloned.1.call-done = bf16[256,512]{1,0:T(8,128)(2,1)} async-done(((bf16[2048,512]{1,0:T(8,128)(2,1)}), bf16[256,512]{1,0:T(8,128)(2,1)}) %reduce-scatter.8.cloned.1.call-update) | async-done | bytes 262160 | tf_op jit(solution)/shard_map/reduce_scatter | solution.py:325
  748.7 156.4 %all-reduce.12.cloned.1.call-done = (bf16[512,2048]{1,0:T(8,128)(2,1)}, bf16[512,2048]{1,0:T(8,128)(2,1)}) async-done(((bf16[512,2048]{1,0:T(8,128)(2,1)}, bf16[512,2048]{1,0:T(8,128)(2,1)}), (bf16[512,2048]{1,0:T(8,128)(2,1)}, bf16[512,2048]{1,0:T(8,128)(2,1)})) %all-reduce.12.cloned.1.call-update) | async-done | bytes 4194320 | tf_op jit(solution)/shard_map/psum | solution.py:255
  908.0 14.7 %all-reduce.2 = (bf16[2048]{0:T(1024)(128)(2,1)S(1)}, bf16[2048]{0:T(1024)(128)(2,1)S(1)}) all-reduce(bf16[2048]{0:T(1024)(128)(2,1)S(1)} %get-tuple-element.338, bf16[2048]{0:T(1024)(128)(2,1)S(1)} %get-tuple-element.336), channel_id=2, replica_groups=mesh['fsdp'=2,'ctx'=4,'tp'=4] {'fsdp','ctx'}, use_global_device_ids=true, to_apply=%region_18.19.clone | all-reduce | flops 4096 | bytes 16384
  923.4 8.0 fusion.61
  931.4 35.6 %reduce-scatter.16.cloned.1.call-done = bf16[256,1408]{1,0:T(8,128)(2,1)} async-done(((bf16[2048,1408]{1,0:T(8,128)(2,1)}), bf16[256,1408]{1,0:T(8,128)(2,1)}) %reduce-scatter.16.cloned.1.call-update) | async-done | bytes 720912 | tf_op jit(solution)/shard_map/reduce_scatter | solution.py:340
  969.3 60.1 %reduce-scatter.18.cloned.1.call-done = bf16[256,1408]{1,0:T(8,128)(2,1)} async-done(((bf16[2048,1408]{1,0:T(8,128)(2,1)}), bf16[256,1408]{1,0:T(8,128)(2,1)}) %reduce-scatter.18.cloned.1.call-update) | async-done | bytes 720912 | tf_op jit(solution)/shard_map/reduce_scatter | solution.py:343
  1031.7 60.4 %reduce-scatter.20.cloned.1.call-done = bf16[1408,256]{1,0:T(8,128)(2,1)} async-done(((bf16[1408,2048]{1,0:T(8,128)(2,1)}), bf16[1408,256]{1,0:T(8,128)(2,1)}) %reduce-scatter.20.cloned.1.call-update) | async-done | bytes 720912 | tf_op jit(solution)/shard_map/reduce_scatter | solution.py:346
  (272 shorter events, 131.2 us)
Async XLA Ops:
  7.2 61.2 %copy-start.1 = (bf16[512,2048]{1,0:T(8,128)(2,1)S(1)}, bf16[512,2048]{1,0:T(8,128)(2,1)}, u32[]{:S(2)}) copy-start(bf16[512,2048]{1,0:T(8,128)(2,1)} %param.17) | copy-start | bytes 6291460
  7.2 88.3 %all-gather.10.cloned.1.call-start = ((), (), s32[]{:S(2)}) async-start(), calls=%async_computation.7 | async-start | bytes 2359296 | tf_op jit(solution)/shard_map/all_gather | solution.py:176
  7.9 146.0 %all-gather.12.cloned.1.call-start = ((), (), s32[]{:S(2)}) async-start(), calls=%async_computation.8 | async-start | bytes 2359296 | tf_op jit(solution)/shard_map/all_gather | solution.py:179
  8.7 238.0 %all-reduce.8.cloned.1.call-start = ((), (), s32[]{:S(2)}) async-start(), calls=%async_computation.9 | async-start | bytes 4194304 | tf_op jit(solution)/shard_map/psum | solution.py:246
  8.7 61.3 %copy-start.37 = (f32[32]{0:T(128)}, f32[32]{0:T(128)S(1)}, u32[]{:S(2)}) copy-start(f32[32]{0:T(128)S(1)} %multiply_power_fusion) | copy-start | bytes 388
  19.1 50.9 %copy-start.32 = (f32[512]{0:T(512)}, f32[512]{0:T(512)S(1)}, u32[]{:S(2)}) copy-start(f32[512]{0:T(512)S(1)} %convert_element_type.186) | copy-start | bytes 6148
  40.4 29.6 %copy-start.24 = (f32[8,1,256]{2,1,0:T(1,128)}, f32[8,1,256]{2,1,0:T(1,128)S(1)}, u32[]{:S(2)}) copy-start(f32[8,1,256]{2,1,0:T(1,128)S(1)} %convert_element_type.230) | copy-start | bytes 24580
  40.4 29.9 %copy-start.36 = (bf16[256,64]{0,1:T(8,128)(2,1)S(1)}, bf16[256,64]{0,1:T(8,128)(2,1)}, u32[]{:S(2)}) copy-start(bf16[256,64]{0,1:T(8,128)(2,1)} %param.21) | copy-start | bytes 98308
  42.5 52.6 %copy-start.30 = (f32[512]{0:T(512)}, f32[512]{0:T(512)S(1)}, u32[]{:S(2)}) copy-start(f32[512]{0:T(512)S(1)} %add_rsqrt_fusion.1) | copy-start | bytes 6148
  68.3 26.8 %copy-start.6 = (bf16[2048,64]{0,1:T(8,128)(2,1)}, bf16[2048,64]{0,1:T(8,128)(2,1)S(1)}, u32[]{:S(2)}) copy-start(bf16[2048,64]{0,1:T(8,128)(2,1)S(1)} %all_gather.34) | copy-start | bytes 786436
  68.3 26.8 %copy-start.20 = (s32[512]{0:T(512)S(1)}, s32[512]{0:T(512)}, u32[]{:S(2)}) copy-start(s32[512]{0:T(512)} %param.28) | copy-start | bytes 6148
  68.3 26.8 %copy-start.22 = (s32[512]{0:T(512)S(1)}, s32[512]{0:T(512)}, u32[]{:S(2)}) copy-start(s32[512]{0:T(512)} %param.29) | copy-start | bytes 6148
  68.9 25.5 %copy-start.2 = (bf16[512,2048]{1,0:T(8,128)(2,1)}, bf16[512,2048]{1,0:T(8,128)(2,1)S(1)}, u32[]{:S(2)}) copy-start(bf16[512,2048]{1,0:T(8,128)(2,1)S(1)} %fusion.67) | copy-start | bytes 6291460
  69.2 29.8 %copy-start.15 = (f32[512,32]{0,1:T(8,128)}, f32[512,32]{0,1:T(8,128)S(1)}, u32[]{:S(2)}) copy-start(f32[512,32]{0,1:T(8,128)S(1)} %get-tuple-element.416) | copy-start | bytes 196612
  69.2 29.8 %copy-start.17 = (f32[512,32]{0,1:T(8,128)}, f32[512,32]{0,1:T(8,128)S(1)}, u32[]{:S(2)}) copy-start(f32[512,32]{0,1:T(8,128)S(1)} %get-tuple-element.417) | copy-start | bytes 196612
  100.2 14.3 %collective-permute-start = (bf16[512,128]{0,1:T(8,128)(2,1)S(1)}, bf16[512,128]{0,1:T(8,128)(2,1)S(1)}, u32[]{:S(2)}, u32[]{:S(2)}) collective-permute-start(bf16[512,128]{0,1:T(8,128)(2,1)S(1)} %copy.50), channel_id=1, source_target_pairs={{0,4},{4,8},{8,12},{12,0},{1,5},{5,9},{9,13},{13,1},{2,6},{6,10},{... | collective-permute-start | bytes 393224 | tf_op jit(solution)/shard_map/while/body/eval_jaxpr/ppermute | solution.py:19
  114.6 16.7 %collective-permute-start = (bf16[512,128]{0,1:T(8,128)(2,1)S(1)}, bf16[512,128]{0,1:T(8,128)(2,1)S(1)}, u32[]{:S(2)}, u32[]{:S(2)}) collective-permute-start(bf16[512,128]{0,1:T(8,128)(2,1)S(1)} %copy.50), channel_id=1, source_target_pairs={{0,4},{4,8},{8,12},{12,0},{1,5},{5,9},{9,13},{13,1},{2,6},{6,10},{... | collective-permute-start | bytes 393224 | tf_op jit(solution)/shard_map/while/body/eval_jaxpr/ppermute | solution.py:19
  131.3 14.2 %collective-permute-start = (bf16[512,128]{0,1:T(8,128)(2,1)S(1)}, bf16[512,128]{0,1:T(8,128)(2,1)S(1)}, u32[]{:S(2)}, u32[]{:S(2)}) collective-permute-start(bf16[512,128]{0,1:T(8,128)(2,1)S(1)} %copy.50), channel_id=1, source_target_pairs={{0,4},{4,8},{8,12},{12,0},{1,5},{5,9},{9,13},{13,1},{2,6},{6,10},{... | collective-permute-start | bytes 393224 | tf_op jit(solution)/shard_map/while/body/eval_jaxpr/ppermute | solution.py:19
  158.3 132.6 %all-gather.14.cloned.1.call-start = ((), (), s32[]{:S(2)}) async-start(), calls=%async_computation.10 | async-start | bytes 6488064 | tf_op jit(solution)/shard_map/all_gather | solution.py:183
  158.9 177.3 %all-gather.16.cloned.1.call-start = ((), (), s32[]{:S(2)}) async-start(), calls=%async_computation.11 | async-start | bytes 6488064 | tf_op jit(solution)/shard_map/all_gather | solution.py:184
  159.5 222.9 %all-gather.18.cloned.1.call-start = ((), (), s32[]{:S(2)}) async-start(), calls=%async_computation.12 | async-start | bytes 6488064 | tf_op jit(solution)/shard_map/all_gather | solution.py:185
  160.1 330.8 %all-reduce.10.cloned.1.call-start = ((), (), s32[]{:S(2)}) async-start(), calls=%async_computation.13 | async-start | bytes 4194304 | tf_op jit(solution)/shard_map/psum | solution.py:266
  174.8 320.0 %copy-start.26 = (f32[8,1,256]{2,1,0:T(1,128)}, f32[8,1,256]{2,1,0:T(1,128)S(1)}, u32[]{:S(2)}) copy-start(f32[8,1,256]{2,1,0:T(1,128)S(1)} %convert_element_type.231) | copy-start | bytes 24580
  249.2 245.6 %copy-start.34 = (f32[512]{0:T(512)}, f32[512]{0:T(512)S(1)}, u32[]{:S(2)}) copy-start(f32[512]{0:T(512)S(1)} %add_rsqrt_fusion) | copy-start | bytes 6148
  392.8 6.6 copy-start.44
  392.8 6.6 copy-start.43
  392.8 6.6 copy-start.39
  404.2 238.8 %reduce-scatter.10.cloned.1.call-start = ((), (), s32[]{:S(2)}) async-start(), calls=%async_computation.15 | async-start | bytes 294912 | tf_op jit(solution)/shard_map/reduce_scatter | solution.py:328
  500.9 84.5 %copy-start.33 = (f32[512]{0:T(512)S(1)}, f32[512]{0:T(512)}, u32[]{:S(2)}) copy-start(f32[512]{0:T(512)} %copy-done.32) | copy-start | bytes 6148
  501.0 84.5 %copy-start.38 = (f32[32]{0:T(128)S(1)}, f32[32]{0:T(128)}, u32[]{:S(2)}) copy-start(f32[32]{0:T(128)} %copy-done.37) | copy-start | bytes 388
  516.1 6.2 collective-permute-start.1
  537.4 5.9 collective-permute-start.1
  558.4 5.9 collective-permute-start.1
  579.5 5.9 collective-permute-start.1
  585.4 6.3 copy-start.27
  585.4 6.3 copy-start.35
  588.6 69.0 %reduce-scatter.12.cloned.1.call-start = ((), (), s32[]{:S(2)}) async-start(), calls=%async_computation.16 | async-start | bytes 294912 | tf_op jit(solution)/shard_map/reduce_scatter | solution.py:331
  591.5 6.9 copy-start.16
  591.5 6.9 copy-start.18
  591.5 110.5 %reduce-scatter.14.cloned.1.call-start = ((), (), s32[]{:S(2)}) async-start(), calls=%async_computation.17 | async-start | bytes 2359296 | tf_op jit(solution)/shard_map/reduce_scatter | solution.py:334
  598.4 148.5 %reduce-scatter.8.cloned.1.call-start = ((), (), s32[]{:S(2)}) async-start(), calls=%async_computation.14 | async-start | bytes 2359296 | tf_op jit(solution)/shard_map/reduce_scatter | solution.py:325
  604.1 301.0 %all-reduce.12.cloned.1.call-start = ((), (), s32[]{:S(2)}) async-start(), calls=%async_computation.21 | async-start | bytes 8388608 | tf_op jit(solution)/shard_map/psum | solution.py:255
  604.1 7.9 copy-start.7
  617.0 350.0 %reduce-scatter.16.cloned.1.call-start = ((), (), s32[]{:S(2)}) async-start(), calls=%async_computation.18 | async-start | bytes 6488064 | tf_op jit(solution)/shard_map/reduce_scatter | solution.py:340
  625.1 404.3 %reduce-scatter.18.cloned.1.call-start = ((), (), s32[]{:S(2)}) async-start(), calls=%async_computation.19 | async-start | bytes 6488064 | tf_op jit(solution)/shard_map/reduce_scatter | solution.py:343
  633.3 458.8 %reduce-scatter.20.cloned.1.call-start = ((), (), s32[]{:S(2)}) async-start(), calls=%async_computation.20 | async-start | bytes 6488064 | tf_op jit(solution)/shard_map/reduce_scatter | solution.py:346
  641.1 264.0 %copy-start.25 = (f32[8,1,256]{2,1,0:T(1,128)S(1)}, f32[8,1,256]{2,1,0:T(1,128)}, u32[]{:S(2)}) copy-start(f32[8,1,256]{2,1,0:T(1,128)} %copy-done.24) | copy-start | bytes 24580
  641.1 264.0 %copy-start.31 = (f32[512]{0:T(512)S(1)}, f32[512]{0:T(512)}, u32[]{:S(2)}) copy-start(f32[512]{0:T(512)} %copy-done.30) | copy-start | bytes 6148
  (21 other events, 66.5 us)
Sparse Core Ops, SparseCore 0:
  9.9 30.6 all-gather.9
  42.5 29.3 all-gather.11
  158.4 88.2 all-reduce.7
  248.6 42.2 all-gather.13
  292.8 43.3 all-gather.15
  338.0 44.3 all-gather.17
  404.3 86.4 all-reduce.9
  588.7 31.8 reduce-scatter.9
  623.9 33.5 reduce-scatter.11
  660.7 41.2 reduce-scatter.13
  705.6 41.2 reduce-scatter.7
  749.7 155.3 all-reduce.11
  908.9 58.0 reduce-scatter.15
  970.3 59.0 reduce-scatter.17
  1033.0 58.9 reduce-scatter.19
where the time goes:
time: 1110 us; the launch traced here: 1100 us
  waiting for transfers between devices  697 us (63%)
  matrix products  188 us (17%)
  blocking collectives  109 us (10%)
  other arithmetic  53.5 us (5%)
  local copies, waits for them, and re-layouts  26.4 us (2%)
  between operations  15.7 us (1%)
    psum x1, waiting for transfers between devices, shards(): lax.psum(project(hidden_low, down_w).astype(jnp.bfloat16), 'tp')  156 us
    psum x1, waiting for transfers between devices, shards(): lax.psum((project_back(gate_grad_low, gate_w) + project_back(up_grad_low,...  85 us
    psum x1, waiting for transfers between devices, shards(): lax.psum(project(attended_low, out_w).astype(jnp.bfloat16), 'tp')  71.9 us
    reduce_scatter x1, waiting for transfers between devices, shards(): lax.psum_scatter(down_w_grad.astype(jnp.bfloat16), ('fsdp', 'ctx'), scatt...  60.4 us
    reduce_scatter x1, waiting for transfers between devices, shards(): lax.psum_scatter(up_w_grad.astype(jnp.bfloat16), ('fsdp', 'ctx'), scatter...  60.1 us
    reduce_scatter x1, waiting for transfers between devices, shards(): lax.psum_scatter(query_w_grad.astype(jnp.bfloat16), ('fsdp', 'ctx'), scat...  43.1 us
    reduce_scatter x1, waiting for transfers between devices, shards(): lax.psum_scatter(out_w_grad.astype(jnp.bfloat16), ('fsdp', 'ctx'), scatte...  43 us
    dot_general x7, matrix products, weight_grad(): lax.dot_general(left_side, right_side, (((0,), (0,)), ((), ())), preferre...  39.9 us
  transfers between devices with their start and end apart: 22, of which 16 were waited for; matrix products, arithmetic and copies ran while one was open for 15% of the time, Pallas kernels for 0%

commit v1 on v0

--- a/solution.py
+++ b/solution.py
@@ -1,6 +1,8 @@
 import jax
 import jax.numpy as jnp
 from jax import lax
+from jax.experimental import pallas as pl
+from jax.experimental.pallas import tpu as pltpu
 from jax.sharding import PartitionSpec as P
 
 H = 32
@@ -350,6 +352,803 @@
     return (output, input_grad) + tuple(summed)
 
 
+MESH = pl.DeviceIdType.MESH
+BF = jnp.bfloat16
+F32 = jnp.float32
+
+
+def dotg(left_side, right_side, left_dim, right_dim):
+    return lax.dot_general(
+        left_side,
+        right_side,
+        (((left_dim,), (right_dim,)), ((), ())),
+        preferred_element_type=F32,
+    )
+
+
+def remote(src, dst, send_sem, recv_sem, device):
+    return pltpu.make_async_remote_copy(
+        src_ref=src,
+        dst_ref=dst,
+        send_sem=send_sem,
+        recv_sem=recv_sem,
+        device_id=device,
+        device_id_type=MESH,
+    )
+
+
+class Place:
+    def __init__(self):
+        self.f = lax.axis_index("fsdp")
+        self.c = lax.axis_index("ctx")
+        self.z = lax.axis_index("tp")
+        self.cx = self.c + 1 - 2 * lax.rem(self.c, 2)
+        self.cy = lax.rem(self.c + 2, 4)
+        self.cd = 3 - self.c
+        self.of = 1 - self.f
+        self.own = self.f * 4 + self.c
+        self.sx = self.f * 4 + self.cx
+        self.sy = self.f * 4 + self.cy
+        self.sd = self.f * 4 + self.cd
+
+    def at(self, f=None, c=None, z=None):
+        return (
+            self.f if f is None else f,
+            self.c if c is None else c,
+            self.z if z is None else z,
+        )
+
+
+def greet(devices):
+    barrier = pltpu.get_barrier_semaphore()
+    for device in devices:
+        pl.semaphore_signal(barrier, inc=1, device_id=device, device_id_type=MESH)
+    pl.semaphore_wait(barrier, len(devices))
+
+
+def group_devices(me):
+    return [
+        me.at(c=me.cx),
+        me.at(c=me.cy),
+        me.at(c=me.cd),
+        me.at(f=me.of),
+        me.at(f=me.of, c=me.cx),
+        me.at(f=me.of, c=me.cy),
+        me.at(f=me.of, c=me.cd),
+    ]
+
+
+def column_devices(me):
+    return [me.at(z=lax.rem(me.z + step, 4)) for step in (1, 2, 3)]
+
+
+class Gather:
+    def __init__(self, me, index, own, full, send, recv, local_sem):
+        self.me, self.own_ref, self.full = me, own, full
+        rows = full.shape[1]
+        self.half_a = pl.ds(0, rows // 2)
+        self.half_b = pl.ds(rows // 2, rows // 2)
+
+        def copy(slot, src, dst, device):
+            return remote(src, dst, send.at[index, slot], recv.at[index, slot], device)
+
+        slot_own, slot_x, slot_y = full.at[me.own], full.at[me.sx], full.at[me.sy]
+        to_x, to_y, to_core = me.at(c=me.cx), me.at(c=me.cy), me.at(f=me.of)
+        diag_a = full.at[me.sd, self.half_a]
+        diag_b = full.at[me.sd, self.half_b]
+        self.own_x = copy(0, own, slot_own, to_x)
+        self.own_y = copy(1, own, slot_own, to_y)
+        self.own_core = copy(2, own, slot_own, to_core)
+        self.pass_x = copy(3, full.at[me.sy, self.half_a], full.at[me.sy, self.half_a], to_x)
+        self.pass_y = copy(4, full.at[me.sx, self.half_b], full.at[me.sx, self.half_b], to_y)
+        self.core_x = copy(5, slot_x, slot_x, to_core)
+        self.core_y = copy(6, slot_y, slot_y, to_core)
+        self.core_a = copy(7, diag_a, diag_a, to_core)
+        self.core_b = copy(8, diag_b, diag_b, to_core)
+        other = me.of * 4
+        into = lambda slot, ref, device: copy(slot, ref, ref, device)
+        self.in_x = into(0, slot_x, to_x)
+        self.in_y = into(1, slot_y, to_y)
+        self.in_a = into(3, diag_a, to_x)
+        self.in_b = into(4, diag_b, to_y)
+        self.in_core = [
+            into(2, full.at[other + me.c], to_core),
+            into(5, full.at[other + me.cx], to_core),
+            into(6, full.at[other + me.cy], to_core),
+            into(7, full.at[other + me.cd, self.half_a], to_core),
+            into(8, full.at[other + me.cd, self.half_b], to_core),
+        ]
+        self.keep = pltpu.make_async_copy(own, slot_own, local_sem.at[index])
+
+    def begin(self):
+        self.own_x.start()
+        self.own_y.start()
+        self.own_core.start()
+        self.keep.start()
+
+    def forward(self):
+        self.in_y.wait_recv()
+        self.pass_x.start()
+        self.core_y.start()
+        self.in_x.wait_recv()
+        self.pass_y.start()
+        self.core_x.start()
+
+    def diagonal(self):
+        self.in_a.wait_recv()
+        self.core_a.start()
+        self.in_b.wait_recv()
+        self.core_b.start()
+
+    def arrive(self):
+        self.keep.wait()
+        for piece in self.in_core:
+            piece.wait_recv()
+
+    def settle(self):
+        for piece in (
+            self.own_x,
+            self.own_y,
+            self.own_core,
+            self.pass_x,
+            self.pass_y,
+            self.core_x,
+            self.core_y,
+            self.core_a,
+            self.core_b,
+        ):
+            piece.wait_send()
+
+
+class LineSum:
+    def __init__(self, me, part, outer_in, inner_in, send, recv):
+        self.me, self.part = me, part
+        self.outer_in, self.inner_in = outer_in, inner_in
+        self.send, self.recv = send, recv
+        z = me.z
+        self.is_mid = (z == 1) | (z == 2)
+        self.is_end = (z == 0) | (z == 3)
+        self.mid_of_end = 1 + z // 3
+        self.outer_of_mid = 3 * (z - 1)
+
+    def end_copies(self):
+        me, part = self.me, self.part
+        mid = self.mid_of_end
+        to_mid = me.at(z=mid)
+        owners = (3 - me.z, 3 - mid, mid)
+        return [
+            remote(
+                part.at[owner],
+                self.outer_in.at[slot],
+                self.send.at[slot],
+                self.recv.at[slot],
+                to_mid,
+            )
+            for slot, owner in enumerate(owners)
+        ]
+
+    def mid_copies(self):
+        me, part = self.me, self.part
+        far_mid, outer = 3 - me.z, self.outer_of_mid
+        far = 3 - outer
+        to_mid, to_outer = me.at(z=far_mid), me.at(z=outer)
+        return [
+            remote(part.at[far], self.inner_in.at[0], self.send.at[0], self.recv.at[3], to_mid),
+            remote(part.at[far_mid], self.inner_in.at[1], self.send.at[1], self.recv.at[4], to_mid),
+            remote(part.at[outer], self.inner_in.at[0], self.send.at[2], self.recv.at[3], to_outer),
+        ]
+
+    def wait_in(self, slot, buffer):
+        remote(buffer, buffer, self.send.at[0], self.recv.at[slot], self.me.at(z=3 - self.me.z)).wait_recv()
+
+    def add(self, owner, buffer):
+        self.part[owner] = (self.part[owner].astype(F32) + buffer[...].astype(F32)).astype(BF)
+
+    def begin(self):
+        @pl.when(self.is_end)
+        def _():
+            for piece in self.end_copies():
+                piece.start()
+
+    def step_one(self):
+        @pl.when(self.is_mid)
+        def _():
+            far = 3 - self.outer_of_mid
+            self.wait_in(0, self.outer_in.at[0])
+            self.add(far, self.outer_in.at[0])
+            self.mid_copies()[0].start()
+
+    def step_two(self):
+        @pl.when(self.is_mid)
+        def _():
+            copies = self.mid_copies()
+            self.wait_in(1, self.outer_in.at[1])
+            self.add(3 - self.me.z, self.outer_in.at[1])
+            copies[1].start()
+            self.wait_in(3, self.inner_in.at[0])
+            self.add(self.outer_of_mid, self.inner_in.at[0])
+            copies[2].start()
+
+    def finish(self, total):
+        me = self.me
+
+        @pl.when(self.is_mid)
+        def _():
+            self.wait_in(2, self.outer_in.at[2])
+            self.wait_in(4, self.inner_in.at[1])
+            total[...] = (
+                self.part[me.z].astype(F32)
+                + self.outer_in[2].astype(F32)
+                + self.inner_in[1].astype(F32)
+            )
+            for piece in self.mid_copies():
+                piece.wait_send()
+
+        @pl.when(self.is_end)
+        def _():
+            self.wait_in(3, self.inner_in.at[0])
+            total[...] = self.part[me.z].astype(F32) + self.inner_in[0].astype(F32)
+            for piece in self.end_copies():
+                piece.wait_send()
+
+
+class LineGather:
+    def __init__(self, me, blocks, send, recv):
+        self.me, self.blocks, self.send, self.recv = me, blocks, send, recv
+        z = me.z
+        self.is_mid = (z == 1) | (z == 2)
+        self.is_end = (z == 0) | (z == 3)
+        self.mid_of_end = 1 + z // 3
+        self.outer_of_mid = 3 * (z - 1)
+
+    def copy(self, owner, slot, z):
+        ref = self.blocks.at[owner]
+        return remote(ref, ref, self.send.at[slot], self.recv.at[owner], self.me.at(z=z))
+
+    def wait_in(self, owner):
+        ref = self.blocks.at[owner]
+        remote(ref, ref, self.send.at[0], self.recv.at[owner], self.me.at(z=3 - self.me.z)).wait_recv()
+
+    def begin(self):
+        me = self.me
+
+        @pl.when(self.is_end)
+        def _():
+            self.copy(me.z, 0, self.mid_of_end).start()
+
+        @pl.when(self.is_mid)
+        def _():
+            self.copy(me.z, 0, self.outer_of_mid).start()
+            self.copy(me.z, 1, 3 - me.z).start()
+
+    def step_one(self):
+        me = self.me
+
+        @pl.when(self.is_mid)
+        def _():
+            self.wait_in(self.outer_of_mid)
+            self.copy(self.outer_of_mid, 2, 3 - me.z).start()
+            self.wait_in(3 - me.z)
+            self.copy(3 - me.z, 3, self.outer_of_mid).start()
+
+    def step_two(self):
+        @pl.when(self.is_mid)
+        def _():
+            far = 3 - self.outer_of_mid
+            self.wait_in(far)
+            self.copy(far, 4, self.outer_of_mid).start()
+
+    def finish(self):
+        me = self.me
+
+        @pl.when(self.is_mid)
+        def _():
+            self.copy(me.z, 0, self.outer_of_mid).wait_send()
+            self.copy(me.z, 1, 3 - me.z).wait_send()
+            self.copy(self.outer_of_mid, 2, 3 - me.z).wait_send()
+            self.copy(3 - me.z, 3, self.outer_of_mid).wait_send()
+            self.copy(3 - self.outer_of_mid, 4, self.outer_of_mid).wait_send()
+
+        @pl.when(self.is_end)
+        def _():
+            mid = self.mid_of_end
+            self.wait_in(mid)
+            self.wait_in(3 - mid)
+            self.wait_in(3 - me.z)
+            self.copy(me.z, 0, mid).wait_send()
+
+
+def row_of(gains_ref, which):
+    return jnp.concatenate([gains_ref[shard, which : which + 1, :] for shard in range(8)], axis=-1)
+
+
+def swap_halves(rows):
+    lane = lax.broadcasted_iota(jnp.int32, rows.shape, 1)
+    return jnp.where(
+        lax.rem(lane, HD) < HD // 2, pltpu.roll(rows, 96, 1), pltpu.roll(rows, 32, 1)
+    )
+
+
+def forward_kernel(
+    tok,
+    w_qkv,
+    w_out,
+    w_gate,
+    w_up,
+    w_down,
+    gains,
+    marks,
+    rope_q,
+    rope_k,
+    f_qkv,
+    f_out,
+    f_gate,
+    f_up,
+    f_down,
+    f_gains,
+    n_one,
+    q_heads,
+    kv_out,
+    bias,
+    lse,
+    att_low,
+    middle,
+    n_two,
+    s_qkv,
+    s_out,
+    s_gains,
+    s_marks,
+    s_kv,
+    s_keys,
+    s_vals,
+    s_qlin,
+    s_part,
+    s_outer,
+    s_inner,
+    s_total,
+    s_blocks,
+    g_send,
+    g_recv,
+    g_local,
+    small_send,
+    small_recv,
+    kv_send,
+    kv_recv,
+    sum_send,
+    sum_recv,
+    all_send,
+    all_recv,
+    out_sem,
+):
+    me = Place()
+    group = group_devices(me)
+    greet(group + column_devices(me))
+
+    qkv = Gather(me, 0, w_qkv, s_qkv, g_send, g_recv, g_local)
+    out = Gather(me, 1, w_out, s_out, g_send, g_recv, g_local)
+    gate = Gather(me, 2, w_gate, f_gate, g_send, g_recv, g_local)
+    up = Gather(me, 3, w_up, f_up, g_send, g_recv, g_local)
+    down = Gather(me, 4, w_down, f_down, g_send, g_recv, g_local)
+
+    small = []
+    for slot, device in enumerate(group):
+        small.append(
+            remote(gains, s_gains.at[me.own], small_send.at[slot], small_recv.at[slot], device)
+        )
+    for slot, device in enumerate(group[:3]):
+        small.append(
+            remote(
+                marks, s_marks.at[me.c], small_send.at[7 + slot], small_recv.at[7 + slot], device
+            )
+        )
+    for piece in small:
+        piece.start()
+    qkv.begin()
+    s_gains[me.own] = gains[...]
+    s_marks[me.c] = marks[...]
+    sources = [me.sx, me.sy, me.sd, me.of * 4 + me.c, me.of * 4 + me.cx, me.of * 4 + me.cy, me.of * 4 + me.cd]
+    for slot, source in enumerate(sources):
+        remote(
+            gains, s_gains.at[source], small_send.at[slot], small_recv.at[slot], group[slot]
+        ).wait_recv()
+    for slot, source in enumerate((me.cx, me.cy, me.cd)):
+        remote(
+            marks, s_marks.at[source], small_send.at[7 + slot], small_recv.at[7 + slot], group[slot]
+        ).wait_recv()
+    f_gains[...] = s_gains[...]
+
+    gain_one = row_of(s_gains, 0)
+
+    def norm_rows(step, carry):
+        rows = pl.ds(pl.multiple_of(step * 64, 64), 64)
+        values = tok[rows, :].astype(F32)
+        inv = lax.rsqrt(jnp.mean(values * values, axis=-1, keepdims=True) + EPSILON)
+        n_one[rows, :] = (values * inv * gain_one).astype(BF)
+        return carry
+
+    lax.fori_loop(0, tok.shape[0] // 64, norm_rows, 0)
+
+    qkv.forward()
+    out.begin()
+    qkv.diagonal()
+
+    def make_bias(group_index):
+        own_rows = marks[:, group_index * 256 : (group_index + 1) * 256].astype(F32)
+        for source in range(4):
+            key_rows = s_marks[source, :, group_index * 256 : (group_index + 1) * 256].astype(F32)
+            key_pos = jnp.transpose(jnp.broadcast_to(key_rows[0:1, :], (128, 256)))
+            key_seg = jnp.transpose(jnp.broadcast_to(key_rows[1:2, :], (128, 256)))
+            for part in range(2):
+                lanes = slice(part * 128, (part + 1) * 128)
+                seen = (key_seg == own_rows[1:2, lanes]) & (key_pos <= own_rows[0:1, lanes])
+                bias[group_index, source * 256 : (source + 1) * 256, lanes] = jnp.where(
+                    seen, 0.0, MASKED_SCORE
+                )
+
+    make_bias(0)
+    make_bias(1)
+    qkv.arrive()
+
+    for first in (0, 256, 512):
+        lanes = slice(first, min(first + 256, 640))
+        total = None
+        for shard in range(8):
+            term = dotg(
+                n_one[:, shard * 256 : (shard + 1) * 256], s_qkv[shard, :, lanes], 1, 0
+            )
+            total = term if total is None else total + term
+        s_qlin[:, lanes] = total
+
+    key_pair = s_qlin[:, 512:640]
+    rot_pair = key_pair * rope_k[:, :128] + swap_halves(key_pair) * rope_k[:, 128:]
+    s_kv[me.c] = rot_pair.astype(BF)
+    kv_copies = [
+        remote(s_kv.at[me.c], s_kv.at[me.c], kv_send.at[slot], kv_recv.at[slot], device)
+        for slot, device in enumerate(group[:3])
+    ]
+    for piece in kv_copies:
+        piece.start()
+    out.forward()
+    for piece in (gate, up, down):
+        piece.begin()
+
+    lane = lax.broadcasted_iota(jnp.int32, (256, 128), 1)
+    for pair in range(4):
+        rows = s_qlin[:, pair * 128 : (pair + 1) * 128]
+        rot = (rows * rope_q[:, :128] + swap_halves(rows) * rope_q[:, 128:]).astype(BF)
+        rot = rot * jnp.bfloat16(HD ** (-0.5))
+        for group_index in range(2):
+            own = rot[group_index * 256 : (group_index + 1) * 256, :]
+            zero = jnp.zeros_like(own)
+            q_heads[group_index * 8 + 2 * pair] = jnp.where(lane < HD, own, zero)
+            q_heads[group_index * 8 + 2 * pair + 1] = jnp.where(lane >= HD, own, zero)
+
+    for slot, source in enumerate((me.cx, me.cy, me.cd)):
+        remote(
+            s_kv.at[source], s_kv.at[source], kv_send.at[slot], kv_recv.at[slot], group[slot]
+        ).wait_recv()
+    lane_kv = lax.broadcasted_iota(jnp.int32, (256, 128), 1)
+    for group_index in range(2):
+        for source in range(4):
+            pairs = s_kv[source, group_index * 256 : (group_index + 1) * 256, :].astype(F32)
+            rows = slice(source * 256, (source + 1) * 256)
+            s_keys[group_index, rows, :] = jnp.where(
+                lane_kv < HD, pairs, pltpu.roll(pairs, HD, 1)
+            ).astype(BF)
+            s_vals[group_index, :, rows] = jnp.transpose(pairs)[HD:, :].astype(BF)
+    kv_out[...] = s_kv[...]
+
+    def attend(step, carry):
+        group_index = step // 4
+        pair = step - group_index * 4
+        halves = []
+        for odd in range(2):
+            head = step * 2 + odd
+            scores = dotg(s_keys[group_index], q_heads[head], 1, 1) + bias[group_index]
+            top = jnp.max(scores, axis=0, keepdims=True)
+            weights = jnp.exp(scores - top)
+            total = jnp.sum(weights, axis=0, keepdims=True)
+            mixed = dotg(s_vals[group_index], weights.astype(BF), 1, 0)
+            halves.append(mixed / total)
+            lse[head] = top + jnp.log(total)
+        rows = jnp.transpose(jnp.concatenate(halves, axis=0))
+        att_low[
+            pl.ds(pl.multiple_of(group_index * 256, 256), 256),
+            pl.ds(pl.multiple_of(pair * 128, 128), 128),
+        ] = rows.astype(BF)
+        return carry
+
+    lax.fori_loop(0, 8, attend, 0)
+
+    out.diagonal()
+    out.arrive()
+    for shard in range(8):
+        lanes = slice(shard * 256, (shard + 1) * 256)
+        s_part[:, :, lanes] = (
+            dotg(att_low[...], s_out[shard], 1, 0).astype(BF).reshape(4, 128, 256)
+        )
+    summed = LineSum(me, s_part, s_outer, s_inner, sum_send, sum_recv)
+    summed.begin()
+    gate.forward()
+    keep = [
+        pltpu.make_async_copy(s_qkv, f_qkv, out_sem.at[0]),
+        pltpu.make_async_copy(s_out, f_out, out_sem.at[1]),
+    ]
+    for piece in keep:
+        piece.start()
+    summed.step_one()
+    up.forward()
+    summed.step_two()
+    summed.finish(s_total)
+
+    own_rows = pl.ds(pl.multiple_of(me.z * 128, 128), 128)
+    mid_rows = tok[own_rows, :].astype(F32) + s_total[...]
+    middle[...] = mid_rows
+    inv_two = lax.rsqrt(jnp.mean(mid_rows * mid_rows, axis=-1, keepdims=True) + EPSILON)
+    s_blocks[me.z] = (mid_rows * inv_two * row_of(s_gains, 1)).astype(BF)
+    spread = LineGather(me, s_blocks, all_send, all_recv)
+    spread.begin()
+    down.forward()
+    gate.diagonal()
+    spread.step_one()
+    up.diagonal()
+    spread.step_two()
+    down.diagonal()
+    gate.arrive()
+    up.arrive()
+    down.arrive()
+    spread.finish()
+    last = pltpu.make_async_copy(s_blocks, n_two, out_sem.at[2])
+    last.start()
+    for piece in small:
+        piece.wait_send()
+    for piece in kv_copies:
+        piece.wait_send()
+    for piece in (qkv, out, gate, up, down):
+        piece.settle()
+    for piece in keep:
+        piece.wait()
+    last.wait()
+
+
+def run_forward(tokens, w_qkv, w_out, w_gate, w_up, w_down, gains, marks, rope_q, rope_k):
+    shape = jax.ShapeDtypeStruct
+    width = tokens.shape[1]
+    hidden = w_gate.shape[1]
+    in_vmem = pl.BlockSpec(memory_space=pltpu.VMEM)
+    anywhere = pl.BlockSpec(memory_space=pl.ANY)
+    dma = pltpu.SemaphoreType.DMA
+    return pl.pallas_call(
+        forward_kernel,
+        name="forward_part",
+        out_shape=(
+            shape((8, 256, 640), BF),
+            shape((8, 512, 256), BF),
+            shape((8, 256, hidden), BF),
+            shape((8, 256, hidden), BF),
+            shape((8, hidden, 256), BF),
+            shape((8, 8, 256), F32),
+            shape((512, width), BF),
+            shape((16, 256, 128), BF),
+            shape((4, 512, 128), BF),
+            shape((2, 1024, 256), F32),
+            shape((16, 1, 256), F32),
+            shape((512, 512), BF),
+            shape((128, width), F32),
+            shape((4, 128, width), BF),
+        ),
+        in_specs=[in_vmem] * 10,
+        out_specs=(anywhere,) * 5 + (in_vmem,) * 8 + (anywhere,),
+        scratch_shapes=[
+            pltpu.VMEM((8, 256, 640), BF),
+            pltpu.VMEM((8, 512, 256), BF),
+            pltpu.VMEM((8, 8, 256), F32),
+            pltpu.VMEM((4, 8, 512), jnp.int32),
+            pltpu.VMEM((4, 512, 128), BF),
+            pltpu.VMEM((2, 1024, 128), BF),
+            pltpu.VMEM((2, HD, 1024), BF),
+            pltpu.VMEM((512, 640), F32),
+            pltpu.VMEM((4, 128, width), BF),
+            pltpu.VMEM((3, 128, width), BF),
+            pltpu.VMEM((2, 128, width), BF),
+            pltpu.VMEM((128, width), F32),
+            pltpu.VMEM((4, 128, width), BF),
+            dma((5, 9)),
+            dma((5, 9)),
+            dma((5,)),
+            dma((10,)),
+            dma((10,)),
+            dma((3,)),
+            dma((3,)),
+            dma((3,)),
+            dma((5,)),
+            dma((5,)),
+            dma((4,)),
+            dma((3,)),
+        ],
+        compiler_params=pltpu.CompilerParams(
+            collective_id=0, has_side_effects=True, vmem_limit_bytes=60000000
+        ),
+    )(tokens, w_qkv, w_out, w_gate, w_up, w_down, gains, marks, rope_q, rope_k)
+
+
+def prepared(tokens, attn_gain, w_query, w_key, w_value, mlp_gain, positions, segments):
+    cosine, sine = rope_tables(positions, HD // 2)
+    one, zero = jnp.ones_like(cosine), jnp.zeros_like(sine)
+    rope_q = jnp.concatenate([cosine] * 4 + [-sine, sine, -sine, sine], axis=-1)
+    rope_k = jnp.concatenate([cosine, cosine, one, one, -sine, sine, zero, zero], axis=-1)
+    w_qkv = jnp.concatenate([w_query, w_key, w_value], axis=1)
+    gains = jnp.pad(jnp.stack([attn_gain, mlp_gain]).astype(F32), ((0, 6), (0, 0)))
+    marks = jnp.pad(jnp.stack([positions, segments]), ((0, 6), (0, 0)))
+    return w_qkv, gains, marks, rope_q, rope_k
+
+
+def fast_shards(
+    tokens,
+    attn_gain,
+    w_query,
+    w_key,
+    w_value,
+    w_out,
+    mlp_gain,
+    w_gate,
+    w_up,
+    w_down,
+    cotangent,
+    positions,
+    segments,
+):
+    token_rows = tokens.shape[0]
+    w_qkv, gains, marks, rope_q, rope_k = prepared(
+        tokens, attn_gain, w_query, w_key, w_value, mlp_gain, positions, segments
+    )
+    (
+        f_qkv, f_out, f_gate, f_up, f_down, f_gains, n_one, q_heads, kv_all, bias, lse, att_low,
+        middle_own, n_two,
+    ) = run_forward(tokens, w_qkv, w_out, w_gate, w_up, w_down, gains, marks, rope_q, rope_k)
+    head_count, kv_heads, groups = 8, 1, 8
+    cosine, sine = rope_tables(positions, HD // 2)
+    query_w = f_qkv.reshape(2048, 640)[:, :512]
+    key_w = f_qkv.reshape(2048, 640)[:, 512:576]
+    value_w = f_qkv.reshape(2048, 640)[:, 576:]
+    out_w = jnp.transpose(f_out, (1, 0, 2)).reshape(512, 2048)
+    down_w = jnp.transpose(f_down, (1, 0, 2)).reshape(-1, 2048)
+    gate_w, up_w = f_gate.reshape(2048, -1), f_up.reshape(2048, -1)
+    gain_one_float = f_gains[:, 0, :].reshape(-1)
+    gain_two_float = f_gains[:, 1, :].reshape(-1)
+    token_float = tokens.astype(jnp.float32)
+    normed_low = n_one
+    inv_one = lax.rsqrt(jnp.mean(token_float * token_float, axis=-1, keepdims=True) + EPSILON)
+    unit_one = token_float * inv_one
+    attended_low = att_low
+    middle = lax.all_gather(middle_own, "tp", axis=0, tiled=True)
+    inv_two = lax.rsqrt(jnp.mean(middle * middle, axis=-1, keepdims=True) + EPSILON)
+    unit_two = middle * inv_two
+    normed_two_low = n_two.reshape(512, 2048)
+    my_index = lax.axis_index("ctx")
+    cycle_size = lax.axis_size("ctx")
+    paired = q_heads.reshape(2, 4, 2, 256, 128)
+    paired = paired[:, :, 0] + paired[:, :, 1]
+    queries = (jnp.transpose(paired, (0, 2, 1, 3)).reshape(512, 1, 8, 64) * 8).astype(jnp.bfloat16)
+    key_positions, key_segments = (
+        lax.all_gather(positions, "ctx", axis=0, tiled=True),
+        lax.all_gather(segments, "ctx", axis=0, tiled=True),
+    )
+    log_total = jnp.transpose(lse.reshape(2, 8, 256), (1, 0, 2)).reshape(1, 8, 512)
+    attended = att_low.astype(jnp.float32).reshape(512, 1, 8, 64)
+
+    def block_marks(source):
+        start_row = source * token_rows
+        return pair_mask(
+            positions,
+            segments,
+            lax.dynamic_slice_in_dim(key_positions, start_row, token_rows),
+            lax.dynamic_slice_in_dim(key_segments, start_row, token_rows),
+        )
+    sources = (my_index - jnp.arange(cycle_size)) % cycle_size
+    kv_blocks = kv_all[sources]
+    kv_local = kv_all[0]
+    gate_lin = project(normed_two_low, gate_w)
+    up_lin = project(normed_two_low, up_w)
+    hidden_low = (jax.nn.silu(gate_lin) * up_lin).astype(jnp.bfloat16)
+    result = middle + lax.psum(project(hidden_low, down_w).astype(jnp.bfloat16), "tp").astype(
+        jnp.float32
+    )
+    output = result.astype(jnp.bfloat16)
+    hidden_grad = project_back(cotangent, down_w)
+    down_w_grad = weight_grad(hidden_low, cotangent)
+    sigmoid_gate = jax.nn.sigmoid(gate_lin)
+    gate_grad_low = (
+        hidden_grad * up_lin * sigmoid_gate * (1.0 + gate_lin * (1.0 - sigmoid_gate))
+    ).astype(jnp.bfloat16)
+    up_grad_low = (hidden_grad * gate_lin * sigmoid_gate).astype(jnp.bfloat16)
+    normed_two_grad = lax.psum(
+        (project_back(gate_grad_low, gate_w) + project_back(up_grad_low, up_w)).astype(
+            jnp.bfloat16
+        ),
+        "tp",
+    ).astype(jnp.float32)
+    gate_w_grad = weight_grad(normed_two_low, gate_grad_low)
+    up_w_grad = weight_grad(normed_two_low, up_grad_low)
+    norm_back_two, gain_two_grad = rms_norm_back(normed_two_grad, gain_two_float, unit_two, inv_two)
+    middle_grad = cotangent.astype(jnp.float32) + norm_back_two
+    middle_low = middle_grad.astype(jnp.bfloat16)
+    attended_grad_low = project_back(middle_low, out_w).astype(jnp.bfloat16)
+    out_w_grad = weight_grad(attended_low, middle_low)
+    out_grad = attended_grad_low.reshape(token_rows, kv_heads, groups, HD)
+    delta_rows = jnp.transpose(jnp.sum(out_grad.astype(jnp.float32) * attended, axis=-1), (1, 2, 0))
+
+    def backward_block(kv_block, source):
+        visible = block_marks(source)
+        return block_grads(queries, out_grad, kv_block, visible, log_total, delta_rows)
+
+    query_start = jnp.zeros((token_rows, kv_heads, groups, HD), jnp.float32)
+
+    def back_step(state_in, pieces):
+        query_acc, kv_acc = state_in
+        query_term, kv_term = backward_block(pieces[0], pieces[1])
+        passed = shifted((kv_acc + kv_term).astype(jnp.bfloat16), "ctx", 1).astype(jnp.float32)
+        return ((query_acc + query_term, passed), None)
+
+    (query_grad, kv_grad), unused = lax.scan(
+        back_step, (query_start, jnp.zeros(kv_local.shape, jnp.float32)), (kv_blocks, sources)
+    )
+    query_grad_low = (
+        rotate_back(query_grad.reshape(token_rows, head_count, HD), cosine, sine)
+        .reshape(token_rows, head_count * HD)
+        .astype(jnp.bfloat16)
+    )
+    key_grad_low = (
+        rotate_back(kv_grad[:, : kv_heads * HD].reshape(token_rows, kv_heads, HD), cosine, sine)
+        .reshape(token_rows, kv_heads * HD)
+        .astype(jnp.bfloat16)
+    )
+    value_grad_low = kv_grad[:, kv_heads * HD :].astype(jnp.bfloat16)
+    normed_one_grad = lax.psum(
+        (
+            project_back(query_grad_low, query_w)
+            + project_back(key_grad_low, key_w)
+            + project_back(value_grad_low, value_w)
+        ).astype(jnp.bfloat16),
+        "tp",
+    ).astype(jnp.float32)
+    query_w_grad = weight_grad(normed_low, query_grad_low)
+    key_w_grad = weight_grad(normed_low, key_grad_low)
+    value_w_grad = weight_grad(normed_low, value_grad_low)
+    norm_back_one, gain_one_grad = rms_norm_back(normed_one_grad, gain_one_float, unit_one, inv_one)
+    input_grad = (middle_grad + norm_back_one).astype(jnp.bfloat16)
+    summed = (
+        lax.psum_scatter(
+            gain_one_grad.astype(jnp.bfloat16), ("fsdp", "ctx"), scatter_dimension=0, tiled=True
+        ).astype(jnp.float32),
+        lax.psum_scatter(
+            query_w_grad.astype(jnp.bfloat16), ("fsdp", "ctx"), scatter_dimension=0, tiled=True
+        ).astype(jnp.float32),
+        lax.psum_scatter(
+            key_w_grad.astype(jnp.bfloat16), ("fsdp", "ctx"), scatter_dimension=0, tiled=True
+        ).astype(jnp.float32),
+        lax.psum_scatter(
+            value_w_grad.astype(jnp.bfloat16), ("fsdp", "ctx"), scatter_dimension=0, tiled=True
+        ).astype(jnp.float32),
+        lax.psum_scatter(
+            out_w_grad.astype(jnp.bfloat16), ("fsdp", "ctx"), scatter_dimension=1, tiled=True
+        ).astype(jnp.float32),
+        lax.psum_scatter(
+            gain_two_grad.astype(jnp.bfloat16), ("fsdp", "ctx"), scatter_dimension=0, tiled=True
+        ).astype(jnp.float32),
+        lax.psum_scatter(
+            gate_w_grad.astype(jnp.bfloat16), ("fsdp", "ctx"), scatter_dimension=0, tiled=True
+        ).astype(jnp.float32),
+        lax.psum_scatter(
+            up_w_grad.astype(jnp.bfloat16), ("fsdp", "ctx"), scatter_dimension=0, tiled=True
+        ).astype(jnp.float32),
+        lax.psum_scatter(
+            down_w_grad.astype(jnp.bfloat16), ("fsdp", "ctx"), scatter_dimension=1, tiled=True
+        ).astype(jnp.float32),
+    )
+    return (output, input_grad) + tuple(summed)
+
+
 def solution(mesh):
     in_specs = (
         P(("fsdp", "ctx"), None),
@@ -379,4 +1178,5 @@
         P(("fsdp", "ctx"), "tp"),
         P("tp", ("fsdp", "ctx")),
     )
-    return jax.shard_map(shards, mesh=mesh, in_specs=in_specs, out_specs=out_specs, check_vma=False)
+    small = (mesh.shape["fsdp"], mesh.shape["ctx"], mesh.shape["tp"]) == (2, 4, 4)
+    return jax.shard_map(fast_shards if small else shards, mesh=mesh, in_specs=in_specs, out_specs=out_specs, check_vma=False)

time: 1110 us -> 938 us (0.85)
  waiting for transfers between devices: 697 us -> 565 us
  Pallas kernels: 0 us -> 131 us
  matrix products: 188 us -> 108 us
  blocking collectives: 109 us -> 30.4 us
  other arithmetic: 53.5 us -> 40.7 us
    pallas_call x0 -> x1, Pallas kernels: none -> 131 us  [run_forward(): pl.pallas_call(forward_kernel, name='forward_part', out_shape=(shape((8,...]
    all_gather x5 -> x1, waiting for transfers between devices: 114 us -> 22.7 us  [fast_shards(): middle = lax.all_gather(middle_own, 'tp', axis=0, tiled=True)]
    all_gather x6 -> x2, blocking collectives: 94.6 us -> 15.6 us  [the longest x1 8.47 us: fast_shards(): lax.all_gather(positions, 'ctx', axis=0, tiled=True)]
    psum x3 -> x2, waiting for transfers between devices: 313 us -> 242 us  [the longest x1 156 us: fast_shards(): lax.psum(project(hidden_low, down_w).astype(jnp.bfloat16), 'tp')]
    dot_general x8 -> x0, matrix products: 30.8 us -> none  [the longest x4 24 us: attend_block(): jnp.einsum('kgqp,pkd->qkgd', weights.astype(jnp.bfloat16), value_rows, pr...]
    reduce_scatter x7, waiting for transfers between devices: 255 us -> 282 us  [the longest x1 61.4 us: fast_shards(): lax.psum_scatter(gate_w_grad.astype(jnp.bfloat16), ('fsdp', 'ctx'), scatt...]
    dot_general x7 -> x3, matrix products: 33.8 us -> 18 us  [project(): return jnp.dot(left_side, right_side, preferred_element_type=jnp.float32)]
    dot_general x7, matrix products: 30.5 us -> 18.9 us  [project_back(): lax.dot_general(left_side, right_side, (((1,), (1,)), ((), ())), preferre...]
  transfers between devices with their start and end apart: 22 -> 14, of which waited for: 16 -> 13; matrix products, arithmetic and copies ran while one was open for 15% -> 11% of each run, Pallas kernels for 0% -> 0%
where the time goes in v1:
time: 938 us; the launch traced here: 930 us
  waiting for transfers between devices  565 us (60%)
  Pallas kernels  131 us (14%)
  matrix products  108 us (12%)
  other arithmetic  40.7 us (4%)
  local copies, waits for them, and re-layouts  32 us (3%)
  blocking collectives  30.4 us (3%)
  between operations  15.8 us (2%)
    psum x1, waiting for transfers between devices, fast_shards(): lax.psum(project(hidden_low, down_w).astype(jnp.bfloat16), 'tp')  156 us
    pallas_call x1, Pallas kernels, run_forward(): pl.pallas_call(forward_kernel, name='forward_part', out_shape=(shape((8,...  131 us
    psum x1, waiting for transfers between devices, fast_shards(): lax.psum((project_back(gate_grad_low, gate_w) + project_back(up_grad_low,...  85.5 us
    reduce_scatter x1, waiting for transfers between devices, fast_shards(): lax.psum_scatter(gate_w_grad.astype(jnp.bfloat16), ('fsdp', 'ctx'), scatt...  61.4 us
    reduce_scatter x1, waiting for transfers between devices, fast_shards(): lax.psum_scatter(down_w_grad.astype(jnp.bfloat16), ('fsdp', 'ctx'), scatt...  60.6 us
    reduce_scatter x1, waiting for transfers between devices, fast_shards(): lax.psum_scatter(up_w_grad.astype(jnp.bfloat16), ('fsdp', 'ctx'), scatter...  60.1 us
    reduce_scatter x1, waiting for transfers between devices, fast_shards(): lax.psum_scatter(query_w_grad.astype(jnp.bfloat16), ('fsdp', 'ctx'), scat...  43.1 us
    reduce_scatter x1, waiting for transfers between devices, fast_shards(): lax.psum_scatter(out_w_grad.astype(jnp.bfloat16), ('fsdp', 'ctx'), scatte...  42.2 us
  transfers between devices with their start and end apart: 14, of which 13 were waited for; matrix products, arithmetic and copies ran while one was open for 11% of the time, Pallas kernels for 0%

profile of v1, /device:TPU:0, one launch (start us, length us, event | category | flops | bytes accessed | tf_op | source)
XLA Modules:
  0.0 929.8 jit_solution(17006965078024500504)
XLA Ops:
  16.7 131.1 %forward_part.1 = (bf16[8,256,640]{2,1,0:T(8,128)(2,1)}, bf16[8,512,256]{2,1,0:T(8,128)(2,1)}, bf16[8,256,1408]{2,1,0:T(8,128)(2,1)}, bf16[8,256,1408]{2,1,0:T(8...) custom-call(bf16[512,2048]{1,0:T(8,128)(2,1)} %tok.1, ...), custom_call_target="tpu_custom_call" | custom-call | tf_op jit(solution)/shard_map/forward_part/pallas_call | solution.py:921
  148.4 8.5 copy.67
  156.9 6.5 fusion.70
  163.5 3.4 fusion.69
  167.0 5.3 multiply_convert_fusion
  172.3 3.4 fusion.71
  175.8 4.7 add_convert_fusion.1
  180.6 2.4 copy.70
  188.1 7.2 all-gather
  195.3 8.5 all-gather.1
  204.7 22.7 %all-gather.4.cloned.1.call-done = f32[512,2048]{1,0:T(8,128)} async-done(((f32[128,2048]{1,0:T(8,128)}), f32[512,2048]{1,0:T(8,128)}) %all-gather.4.cloned.1.call-update) | async-done | bytes 4194320 | tf_op jit(solution)/shard_map/all_gather | solution.py:1024
  227.4 2.5 multiply_reduce_fusion
  230.0 85.5 %all-reduce.9.cloned.1.call-done = bf16[512,2048]{1,0:T(8,128)(2,1)} async-done(((bf16[512,2048]{1,0:T(8,128)(2,1)}), bf16[512,2048]{1,0:T(8,128)(2,1)}) %all-reduce.9.cloned.1.call-update) | async-done | bytes 2097168 | tf_op jit(solution)/shard_map/psum | solution.py:1065
  315.4 4.2 fusion.37
  320.1 3.1 fusion.36
  325.4 64.0 %while.13 = (s32[]{:T(128)}, f32[512,1,8,64]{0,3,2,1:T(8,128)S(1)}, f32[512,128]{0,1:T(8,128)S(1)}, bf16[4,512,128]{2,1,0:T(8,128)(2,1)S(1)}, s32[512]{0:T(512)S...) while((s32[]{:T(128)}, f32[512,1,8,64]{0,3,2,1:T(8,128)S(1)}, ...), condition=%wide.region_7.8_spmd.clone, body=%wide.region_6.7_spmd.clone.sunk | while | flops 1369276416 | bytes 47448368 | solution.py:1093
  328.5 2.4 fusion.122
  330.8 3.1 fusion.120
  337.8 3.8 collective-permute-done
  344.7 2.4 fusion.122
  347.1 3.1 fusion.120
  353.1 4.4 collective-permute-done
  360.7 2.4 fusion.122
  363.0 3.1 fusion.120
  368.5 4.9 collective-permute-done
  376.6 2.4 fusion.122
  379.0 3.1 fusion.120
  384.4 4.9 collective-permute-done
  389.5 2.9 convolution_convert_fusion.6
  392.7 2.8 convolution_convert_fusion.7
  395.8 7.6 convolution_convert_fusion.2
  405.0 6.6 convolution_convert_fusion.1
  413.2 6.4 convolution_convert_fusion
  420.6 4.8 convolution_convert_fusion.3
  425.9 4.2 convolution_convert_fusion.4
  430.5 8.0 convolution_convert_fusion.5
  446.5 15.0 %reduce-scatter.10.cloned.1.call-done = bf16[256,64]{0,1:T(8,128)(2,1)} async-done(((bf16[2048,64]{0,1:T(8,128)(2,1)}), bf16[256,64]{0,1:T(8,128)(2,1)}) %reduce-scatter.10.cloned.1.call-update) | async-done | bytes 32784 | tf_op jit(solution)/shard_map/reduce_scatter | solution.py:1127
  462.9 61.4 %reduce-scatter.16.cloned.1.call-done = bf16[256,1408]{1,0:T(8,128)(2,1)} async-done(((bf16[2048,1408]{1,0:T(8,128)(2,1)}), bf16[256,1408]{1,0:T(8,128)(2,1)}) %reduce-scatter.16.cloned.1.call-update) | async-done | bytes 720912 | tf_op jit(solution)/shard_map/reduce_scatter | solution.py:1139
  526.6 60.1 %reduce-scatter.18.cloned.1.call-done = bf16[256,1408]{1,0:T(8,128)(2,1)} async-done(((bf16[2048,1408]{1,0:T(8,128)(2,1)}), bf16[256,1408]{1,0:T(8,128)(2,1)}) %reduce-scatter.18.cloned.1.call-update) | async-done | bytes 720912 | tf_op jit(solution)/shard_map/reduce_scatter | solution.py:1142
  586.6 2.3 convert_element_type.173
  589.0 60.6 %reduce-scatter.20.cloned.1.call-done = bf16[1408,256]{1,0:T(8,128)(2,1)} async-done(((bf16[1408,2048]{1,0:T(8,128)(2,1)}), bf16[1408,256]{1,0:T(8,128)(2,1)}) %reduce-scatter.20.cloned.1.call-update) | async-done | bytes 720912 | tf_op jit(solution)/shard_map/reduce_scatter | solution.py:1145
  649.5 2.3 convert_element_type.175
  651.8 42.2 %reduce-scatter.14.cloned.1.call-done = bf16[512,256]{1,0:T(8,128)(2,1)} async-done(((bf16[512,2048]{1,0:T(8,128)(2,1)}), bf16[512,256]{1,0:T(8,128)(2,1)}) %reduce-scatter.14.cloned.1.call-update) | async-done | bytes 262160 | tf_op jit(solution)/shard_map/reduce_scatter | solution.py:1133
  695.8 43.1 %reduce-scatter.8.cloned.1.call-done = bf16[256,512]{1,0:T(8,128)(2,1)} async-done(((bf16[2048,512]{1,0:T(8,128)(2,1)}), bf16[256,512]{1,0:T(8,128)(2,1)}) %reduce-scatter.8.cloned.1.call-update) | async-done | bytes 262160 | tf_op jit(solution)/shard_map/reduce_scatter | solution.py:1124
  740.7 156.4 %all-reduce.11.cloned.1.call-done = (bf16[512,2048]{1,0:T(8,128)(2,1)}, bf16[512,2048]{1,0:T(8,128)(2,1)}) async-done(((bf16[512,2048]{1,0:T(8,128)(2,1)}, bf16[512,2048]{1,0:T(8,128)(2,1)}), (bf16[512,2048]{1,0:T(8,128)(2,1)}, bf16[512,2048]{1,0:T(8,128)(2,1)})) %all-reduce.11.cloned.1.call-update) | async-done | bytes 4194320 | tf_op jit(solution)/shard_map/psum | solution.py:1054
  897.1 2.9 fusion.40
  900.1 14.7 %all-reduce.4 = (bf16[2048]{0:T(1024)(128)(2,1)S(1)}, bf16[2048]{0:T(1024)(128)(2,1)S(1)}) all-reduce(bf16[2048]{0:T(1024)(128)(2,1)S(1)} %get-tuple-element.203, bf16[2048]{0:T(1024)(128)(2,1)S(1)} %get-tuple-element.201), channel_id=2, replica_groups=mesh['fsdp'=2,'ctx'=4,'tp'=4] {'fsdp','ctx'}, use_global_device_ids=true, to_apply=%region_11.12.clone | all-reduce | flops 4096 | bytes 16384
  915.4 7.1 fusion.33
  (192 shorter events, 60.9 us)
Async XLA Ops:
  7.2 7.5 copy-start.17
  7.2 7.5 copy-start.18
  7.2 8.7 copy-start.16
  7.2 220.2 %all-gather.4.cloned.1.call-start = ((), (), s32[]{:S(2)}) async-start(), calls=%async_computation.7 | async-start | bytes 5242880 | tf_op jit(solution)/shard_map/all_gather | solution.py:1024
  12.1 135.7 %copy-start.3 = (f32[512,32]{1,0:T(8,128)}, f32[512,32]{1,0:T(8,128)S(1)}, u32[]{:S(2)}) copy-start(f32[512,32]{1,0:T(8,128)S(1)} %get-tuple-element.246) | copy-start | bytes 196612
  12.1 135.7 %copy-start.6 = (f32[512,32]{1,0:T(8,128)}, f32[512,32]{1,0:T(8,128)S(1)}, u32[]{:S(2)}) copy-start(f32[512,32]{1,0:T(8,128)S(1)} %get-tuple-element.244) | copy-start | bytes 196612
  147.8 167.6 %all-reduce.9.cloned.1.call-start = ((), (), s32[]{:S(2)}) async-start(), calls=%async_computation.8 | async-start | bytes 4194304 | tf_op jit(solution)/shard_map/psum | solution.py:1065
  148.4 15.1 %slice-start.4 = ((s8[5767168]{0:T(1024)(128)(4,1)}), s8[1572864]{0:T(1024)(128)(4,1)S(1)}, s32[]{:S(2)}) async-start(s8[5767168]{0:T(1024)(128)(4,1)} %bitcast.225), calls=%async_computation.21 | async-start | bytes 3145728
  156.9 6.6 slice-start.5
  156.9 6.6 copy-start.20
  156.9 10.1 %slice-start = ((s8[5767168]{0:T(1024)(128)(4,1)}), s8[4194304]{0:T(1024)(128)(4,1)S(1)}, s32[]{:S(2)}) async-start(s8[5767168]{0:T(1024)(128)(4,1)} %bitcast.191), calls=%async_computation.17 | async-start | bytes 8388608
  163.4 3.5 slice-start.1
  163.5 3.5 copy-start.9
  163.5 12.3 %slice-start.2 = ((s8[5767168]{0:T(1024)(128)(4,1)}), s8[4194304]{0:T(1024)(128)(4,1)S(1)}, s32[]{:S(2)}) async-start(s8[5767168]{0:T(1024)(128)(4,1)} %bitcast.222), calls=%async_computation.19 | async-start | bytes 8388608
  167.0 8.8 slice-start.3
  172.3 3.5 copy-start.24
  172.3 3.5 copy-start.23
  175.8 4.8 copy-start.11
  180.5 264.6 %reduce-scatter.12.cloned.1.call-start = ((), (), s32[]{:S(2)}) async-start(), calls=%async_computation.11 | async-start | bytes 294912 | tf_op jit(solution)/shard_map/reduce_scatter | solution.py:1130
  180.6 5.8 copy-start.19
  315.4 4.2 copy-start
  315.4 4.7 copy-start.5
  320.1 3.1 copy-start.12
  323.2 2.0 copy-start.2
  324.5 0.9 copy-start.14
  326.9 1.6 copy-start.15
  335.3 6.2 collective-permute-start
  343.1 1.6 copy-start.15
  351.6 5.9 collective-permute-start
  359.1 1.6 copy-start.15
  367.5 5.9 collective-permute-start
  375.0 1.6 copy-start.15
  383.5 5.9 collective-permute-start
  389.4 6.4 copy-start.25
  392.4 69.1 %reduce-scatter.10.cloned.1.call-start = ((), (), s32[]{:S(2)}) async-start(), calls=%async_computation.10 | async-start | bytes 294912 | tf_op jit(solution)/shard_map/reduce_scatter | solution.py:1127
  395.5 128.7 %reduce-scatter.16.cloned.1.call-start = ((), (), s32[]{:S(2)}) async-start(), calls=%async_computation.13 | async-start | bytes 6488064 | tf_op jit(solution)/shard_map/reduce_scatter | solution.py:1139
  403.4 1.6 copy-start.21
  403.4 183.2 %reduce-scatter.18.cloned.1.call-start = ((), (), s32[]{:S(2)}) async-start(), calls=%async_computation.14 | async-start | bytes 6488064 | tf_op jit(solution)/shard_map/reduce_scatter | solution.py:1142
  411.6 1.6 copy-start.10
  411.6 237.9 %reduce-scatter.20.cloned.1.call-start = ((), (), s32[]{:S(2)}) async-start(), calls=%async_computation.15 | async-start | bytes 6488064 | tf_op jit(solution)/shard_map/reduce_scatter | solution.py:1145
  419.6 1.0 copy-start.13
  419.6 5.9 copy-start.4
  419.6 6.0 copy-start.7
  419.6 274.4 %reduce-scatter.14.cloned.1.call-start = ((), (), s32[]{:S(2)}) async-start(), calls=%async_computation.12 | async-start | bytes 2359296 | tf_op jit(solution)/shard_map/reduce_scatter | solution.py:1133
  425.5 313.5 %reduce-scatter.8.cloned.1.call-start = ((), (), s32[]{:S(2)}) async-start(), calls=%async_computation.9 | async-start | bytes 2359296 | tf_op jit(solution)/shard_map/reduce_scatter | solution.py:1124
  430.2 8.3 copy-start.8
  430.2 466.9 %all-reduce.11.cloned.1.call-start = ((), (), s32[]{:S(2)}) async-start(), calls=%async_computation.16 | async-start | bytes 8388608 | tf_op jit(solution)/shard_map/psum | solution.py:1054
  442.7 1.9 copy-start.1
  (1 other events, 0.7 us)
Sparse Core Ops, SparseCore 0:
  148.0 79.4 all-gather.3
  230.3 85.0 all-reduce.8
  392.5 31.8 reduce-scatter.11
  427.8 33.6 reduce-scatter.9
  465.2 59.0 reduce-scatter.15
  527.6 59.0 reduce-scatter.17
  590.5 58.9 reduce-scatter.19
  652.8 41.2 reduce-scatter.13
  697.7 41.2 reduce-scatter.7
  741.8 155.3 all-reduce.10
